TPU v7x, 256 devices: a whole 4x4x8 slice. The times are simulated.
256 devices in a mesh: scan: 4 (over y), slab: 64 (over z, x, core).
Axes of the slice: x: 4, y: 4, z: 8, core: 2. Of those that a mesh axis runs over, the one named last changes fastest.
Arguments:
- volume: float32 [4, 32768, 1024], P('scan', 'slab'), may hold values from -108 to 108
- velocity0: float32 [4, 32768], P('scan', 'slab'), may hold values from -0.5 to 0.5
- fetch_slab: int32 [4, 2, 32768, 1], P('scan', None, 'slab'), may hold values from 0 to 63; in each aligned block of 512 rows (0 to 511, 512 to 1023, ..., all dimensions but the last counted through in order) at most 12 rows name the same one
- fetch_row: int32 [4, 2, 32768], P('scan', None, 'slab'), may hold values from 0 to 511
- modulus_class: int32 [4, 32768], P('scan', 'slab'), may hold values from 0 to 3
- modulus_table: float32 [4], replicated, may hold values from 200 to 3000
Outputs:
- velocity: float32 [4, 32768], P('scan', 'slab')
- misfit: float32 [4, 32768, 1024], P('scan', 'slab')
Inputs may be any that keep to these rules, and one draw needn't show every extreme that they name: `fetch_slab`: among the rows of one device for one direction, at most 12 name the same slab, a bound that some block reaches of them.
All inputs are finite; a program needn't handle non-finite values.
Results may differ from a plain program's by a relative error of at most 0.00011.
Values sent between devices are 32-bit elements; how exact they have to be, the bound alone decides.
A program may use at most 64 MiB of HBM per device.

v0:
```python
import math
import jax
import jax.numpy as jnp
from jax import lax
from jax.sharding import PartitionSpec as P

Y = 1024
BAND = 32
ITERS = 2
root_three = math.sqrt(3.0)
pole_value = math.sqrt(3.0) - 2.0


def with_halo(cells, sides, width):
    for axis, dim in sides:
        count = lax.axis_size(axis)
        ends = count - 1
        head = lax.slice_in_dim(cells, 0, width, axis=dim)
        tail = lax.slice_in_dim(cells, cells.shape[dim] - width, cells.shape[dim], axis=dim)
        cells = jnp.concatenate(
            [
                lax.ppermute(tail, axis, [(i, (i + 1) % count) for i in range(ends)]),
                cells,
                lax.ppermute(head, axis, [((i + 1) % count, i) for i in range(ends)]),
            ],
            axis=dim,
        )
    return cells


def passed_along(block, axis, distance):
    devices = range(lax.axis_size(axis))
    route = [(i - distance, i) for i in devices if i - distance in devices]
    return lax.ppermute(block, axis, route)


def filter_block(block_width, band_reach):
    offsets = (
        lax.broadcasted_iota(jnp.int32, (3 * block_width, block_width), 0)
        - block_width
        - lax.broadcasted_iota(jnp.int32, (3 * block_width, block_width), 1)
    )
    distance = jnp.abs(offsets)
    parity = 1.0 - 2.0 * (distance % 2).astype(jnp.float32)
    magnitude = jnp.exp(distance.astype(jnp.float32) * math.log(-pole_value))
    return jnp.where(
        distance <= band_reach, root_three * parity * magnitude, jnp.zeros_like(magnitude)
    )


def prefilter(voxels):
    length = voxels.shape[1]
    block_width = min(128, length)
    matrix = filter_block(block_width, BAND)
    padded = jnp.pad(voxels, ((0, 0), (block_width, block_width)))
    pieces = []
    for number in range(length // block_width):
        window = padded[:, number * block_width : number * block_width + 3 * block_width]
        pieces.append(
            jnp.dot(
                window, matrix, preferred_element_type=jnp.float32, precision=lax.Precision.HIGHEST
            )
        )
    return jnp.concatenate(pieces, axis=1)


def taylor_terms(coeffs):
    padded = jnp.pad(coeffs, ((0, 0), (1, 1)))
    before = padded[:, :-2]
    after = padded[:, 2:]
    value = (before + 4.0 * coeffs + after) / 6.0
    slope = 0.5 * (after - before)
    bend = after - 2.0 * coeffs + before
    return (value, slope, bend)


def residuals(forward, backward, voxels, velocity):
    moved = velocity[:, None]
    fwd_value, fwd_slope, fwd_bend = taylor_terms(forward)
    bwd_value, bwd_slope, bwd_bend = taylor_terms(backward)
    res_fwd = fwd_value + moved * fwd_slope + 0.5 * moved * moved * fwd_bend - voxels
    jac_fwd = fwd_slope + moved * fwd_bend
    res_bwd = bwd_value - moved * bwd_slope + 0.5 * moved * moved * bwd_bend - voxels
    jac_bwd = moved * bwd_bend - bwd_slope
    return (res_fwd, jac_fwd, res_bwd, jac_bwd)


def row_terms(forward, backward, voxels, velocity):
    res_fwd, jac_fwd, res_bwd, jac_bwd = residuals(forward, backward, voxels, velocity)
    linear = jnp.sum(jac_fwd * res_fwd + jac_bwd * res_bwd, axis=1)
    curvature = jnp.sum(jac_fwd * jac_fwd + jac_bwd * jac_bwd, axis=1)
    return (linear, curvature)


def plane_stencil(field):
    count_rows = field.shape[0]
    hops = Y // count_rows
    rimmed = with_halo(field[None, :], (("slab", 1),), 1)[0]
    lower = passed_along(field, "slab", hops)
    upper = passed_along(field, "slab", -hops)
    return 4.0 * field - rimmed[:-2] - rimmed[2:] - lower - upper


def on_device(volume, velocity0, fetch_slab, fetch_row, modulus_class, modulus_table):
    own_scan = volume[0]
    count_rows = own_scan.shape[0]
    devices = lax.axis_size("slab")
    capacity = max(2, 3 * count_rows // (2 * devices))
    ahead_rows = passed_along(own_scan, "scan", -1)
    behind = passed_along(own_scan, "scan", 1)
    peer_ids = fetch_slab[0, :, :, 0]
    wanted_rows = fetch_row[0]
    one_hot = (peer_ids[:, :, None] == lax.broadcasted_iota(jnp.int32, (1, 1, devices), 2)).astype(
        jnp.int32
    )
    running = jnp.cumsum(one_hot, axis=1) - one_hot
    slot_ids = jnp.sum(running * one_hot, axis=2)
    direction_ids = lax.broadcasted_iota(jnp.int32, (2, count_rows), 0)
    request_table = (
        jnp.zeros((2, devices, capacity), jnp.int32)
        .at[direction_ids, peer_ids, slot_ids]
        .set(wanted_rows)
    )
    asked_rows = lax.all_to_all(request_table, "slab", split_axis=1, concat_axis=1, tiled=True)
    forward_rows = jnp.take(ahead_rows, asked_rows[0], axis=0)
    backward_rows = jnp.take(behind, asked_rows[1], axis=0)
    arrived = lax.all_to_all(
        jnp.stack([forward_rows, backward_rows]), "slab", split_axis=1, concat_axis=1, tiled=True
    )
    fetched = arrived[direction_ids, peer_ids, slot_ids]
    filtered = prefilter(fetched.reshape(2 * count_rows, fetched.shape[2]))
    forward = filtered[:count_rows]
    backward = filtered[count_rows:]
    classes = lax.broadcasted_iota(jnp.int32, (1, modulus_table.shape[0]), 1)
    weight = jnp.sum(
        jnp.where(
            modulus_class[0][:, None] == classes,
            modulus_table[None, :],
            jnp.zeros_like(modulus_table)[None, :],
        ),
        axis=1,
    )
    stiffness = jnp.sqrt(weight)
    velocity = velocity0[0]
    for iteration in range(ITERS):
        linear, curvature = row_terms(forward, backward, own_scan, velocity)
        gradient = linear + stiffness * plane_stencil(stiffness * velocity)
        diagonal = curvature + 4.0 * stiffness * stiffness
        direction = gradient / diagonal
        scaled_dir = stiffness * direction
        bend_term = scaled_dir * plane_stencil(scaled_dir)
        totals = lax.psum(
            (jnp.sum(direction * gradient), jnp.sum(curvature * direction * direction + bend_term)),
            ("scan", "slab"),
        )
        velocity = velocity - totals[0] / totals[1] * direction
    res_fwd, jac_fwd, res_bwd, jac_bwd = residuals(forward, backward, own_scan, velocity)
    return (velocity[None, :], (res_fwd + res_bwd)[None])


def solution(mesh):
    return jax.shard_map(
        on_device,
        mesh=mesh,
        in_specs=(
            P("scan", "slab", None),
            P("scan", "slab"),
            P("scan", None, "slab", None),
            P("scan", None, "slab"),
            P("scan", "slab"),
            P(),
        ),
        out_specs=(P("scan", "slab"), P("scan", "slab", None)),
        check_vma=False,
    )
```

profile of v0, /device:TPU:1, one launch (start us, length us, event | category | flops | bytes accessed | tf_op | source)
XLA Modules:
  0.0 537.1 jit_solution(10035754950157322251)
XLA Ops:
  0.7 2.9 copy.63
  3.6 1.3 collective-permute-start
  4.9 6.0 %collective-permute-start.1 = (f32[512,1024]{0,1:T(8,128)}, f32[512,1024]{0,1:T(8,128)}, u32[]{:S(2)}, u32[]{:S(2)}) collective-permute-start(f32[512,1024]{0,1:T(8,128)} %bitcast.6), channel_id=1, source_target_pairs={{0,64},{64,128},{128,192},{1,65},{65,129},{129,193},{2,66},{66,130... | collective-permute-start | bytes 6291464 | tf_op jit(solution)/shard_map/ppermute | solution.py:34
  10.9 2.4 reduce-window.6
  13.3 0.3 slice_reduce_fusion
  14.2 4.3 scatter_custom_fusion
  18.7 23.1 %all_to_all.10 = s32[2,64,12]{2,0,1:T(2,128)S(1)} all-to-all(s32[2,64,12]{2,0,1:T(2,128)S(1)} %copy.60), channel_id=1, replica_groups=mesh['scan'=4,'slab'=64] {'slab'}, dimensions={1} | all-to-all | bytes 12288 | tf_op jit(solution)/shard_map/all_to_all | solution.py:124
  42.7 8.4 %collective-permute-done = f32[512,1024]{0,1:T(8,128)} collective-permute-done((f32[512,1024]{0,1:T(8,128)}, f32[512,1024]{0,1:T(8,128)}, u32[]{:S(2)}, u32[]{:S(2)}) %collective-permute-start) | collective-permute-done | bytes 2097184 | tf_op jit(solution)/shard_map/ppermute | solution.py:34
  51.1 1.9 copy.65
  53.0 3.6 gather_fusion.1
  56.6 4.6 reshape.161
  61.2 1.9 copy.69
  63.1 3.7 gather_fusion.2
  66.8 4.6 reshape.165
  71.4 3.8 select_bitcast_fusion
  75.3 4.2 pad_maximum_fusion
  79.5 12.0 %copy.70 = f32[2,64,12,1024]{3,0,2,1:T(2,128)} copy(f32[2,64,12,1024]{3,2,1,0:T(8,128)} %pad_maximum_fusion) | data formatting | bytes 12582912 | tf_op jit(solution)/shard_map/stack | solution.py:128
  91.4 15.3 %all-to-all-start.1 = ((f32[2,64,12,1024]{3,0,2,1:T(2,128)}), f32[2,64,12,1024]{3,0,2,1:T(2,128)}, u32[]{:S(2)}, u32[]{:S(2)}) async-start(f32[2,64,12,1024]{3,0,2,1:T(2,128)} %copy.70), calls=%async_computation.1 | async-start | bytes 12582912 | tf_op jit(solution)/shard_map/all_to_all | solution.py:127
  106.9 3.3 collective-permute-start.4
  110.1 1.3 collective-permute-start.5
  111.5 0.6 fusion.144
  112.0 4.8 collective-permute-start.2
  116.9 13.8 %collective-permute-start.3 = (f32[1,1]{1,0:T(1,128)}, f32[1,1]{1,0:T(1,128)}, u32[]{:S(2)}, u32[]{:S(2)}) collective-permute-start(f32[1,1]{1,0:T(1,128)} %get-tuple-element.67), channel_id=1, source_target_pairs={{1,0},{2,1},{3,2},{4,3},{5,4},{6,5},{7,6},{8,7},{9,8},{10,9},{11,1... | collective-permute-start | bytes 20 | tf_op jit(solution)/shard_map/ppermute | solution.py:24
  130.7 1.3 pad_maximum_fusion.8
  132.1 113.6 %all-to-all-done.1 = f32[2,64,12,1024]{3,0,2,1:T(2,128)} async-done(((f32[2,64,12,1024]{3,0,2,1:T(2,128)}), f32[2,64,12,1024]{3,0,2,1:T(2,128)}, u32[]{:S(2)}, u32[]{:S(2)}) %all-to-all-start.1) | async-done | bytes 6291488 | tf_op jit(solution)/shard_map/all_to_all | solution.py:127
  245.6 9.1 %copy.71 = f32[2,64,12,1024]{3,1,2,0:T(8,128)} copy(f32[2,64,12,1024]{3,0,2,1:T(2,128)} %all-to-all-done.1) | data formatting | bytes 12582912 | tf_op jit(solution)/shard_map/all_to_all | solution.py:127
  254.7 21.5 %gather_fusion = f32[1024,1024]{1,0:T(8,128)} fusion(f32[2,64,12,1024]{3,1,2,0:T(8,128)} %copy.71, s32[1024]{0:T(1024)S(1)} %bitcast.67), kind=kCustom, calls=%fused_computation.2 | custom fusion | bytes 8400896 | tf_op jit(solution)/shard_map/gather | solution.py:130
  276.2 3.3 fusion.35
  279.5 2.0 fusion.16
  281.5 2.0 fusion.19
  283.5 2.0 fusion.22
  285.4 2.0 fusion.25
  287.4 2.0 fusion.28
  289.4 2.0 fusion.31
  291.3 2.0 fusion.34
  293.3 0.5 fusion.139
  293.9 7.1 %add_reduce_fusion.2 = (f32[512]{0:T(512)S(1)}, f32[512]{0:T(512)S(1)}, f32[512,1024]{0,1:T(8,128)S(1)}, f32[512,1024]{0,1:T(8,128)}, f32[512,1024]{0,1:T(8,128)...) fusion(f32[512]{0:T(512)S(1)} %bitcast.69, f32[1,512,1024]{1,2,0:T(8,128)} %copy.63, ...), kind=kLoop, calls=%fused_computation.14 | loop fusion | flops 20970496 | bytes 18884608 | tf_op jit(solution)/shard_map/reduce_sum | solution.py:91
  301.0 3.1 collective-permute-start.8
  304.1 1.3 collective-permute-start.9
  305.4 0.6 fusion.143
  306.0 7.2 %collective-permute-start.6 = (f32[1,1]{1,0:T(1,128)}, f32[1,1]{1,0:T(1,128)}, u32[]{:S(2)}, u32[]{:S(2)}) collective-permute-start(f32[1,1]{1,0:T(1,128)} %get-tuple-element.62), channel_id=1, source_target_pairs={{0,1},{1,2},{2,3},{3,4},{4,5},{5,6},{6,7},{7,8},{8,9},{9,10},{10,1... | collective-permute-start | bytes 20 | tf_op jit(solution)/shard_map/ppermute | solution.py:22
  313.3 1.9 collective-permute-start.7
  315.2 3.3 collective-permute-done.7
  318.5 1.4 pad_maximum_fusion.6
  319.8 0.6 fusion.59
  320.5 78.0 %all-reduce.4 = (f32[]{:T(128)}, f32[]{:T(128)}) all-reduce(f32[]{:T(128)} %get-tuple-element.22, f32[]{:T(128)} %get-tuple-element.21), channel_id=1, replica_groups=mesh['scan'=4,'slab'=64] {'scan','slab'}, use_global_device_ids=true, to_apply=%region_8.10 | all-reduce | flops 2 | bytes 16 | tf_op jit(solution)/shard_map/psum | solution.py:152
  399.8 2.6 collective-permute-start.12
  402.4 1.3 collective-permute-start.13
  403.7 0.6 fusion.142
  404.3 5.1 collective-permute-start.10
  409.4 1.9 collective-permute-start.11
  411.4 5.5 %add_reduce_fusion = (f32[512]{0:T(512)S(1)}, f32[512]{0:T(512)S(1)}) fusion(f32[512,1024]{0,1:T(8,128)} %get-tuple-element.42, f32[512,1024]{0,1:T(8,128)} %get-tuple-element.41, f32[512,1024]{0,1:T(8,128)} %get-tuple-element.40, f32[512,1024]{0,1:T(8,128)} %get-tuple-element.39, f32[512]{0:T(512)S(1)} %get-tuple-element.33, ...), kind=kLoop, calls=%fused_computation.10 | loop fusion | flops 12581888 | bytes 14690304 | tf_op jit(solution)/shard_map/reduce_sum | solution.py:91
  416.9 1.4 pad_maximum_fusion.4
  418.3 2.2 collective-permute-start.16
  420.6 1.3 collective-permute-start.17
  421.9 0.6 fusion.141
  422.4 5.9 %collective-permute-start.14 = (f32[1,1]{1,0:T(1,128)}, f32[1,1]{1,0:T(1,128)}, u32[]{:S(2)}, u32[]{:S(2)}) collective-permute-start(f32[1,1]{1,0:T(1,128)} %get-tuple-element.52), channel_id=1, source_target_pairs={{0,1},{1,2},{2,3},{3,4},{4,5},{5,6},{6,7},{7,8},{8,9},{9,10},{10,1... | collective-permute-start | bytes 20 | tf_op jit(solution)/shard_map/ppermute | solution.py:22
  428.4 1.9 collective-permute-start.15
  430.3 3.3 collective-permute-done.15
  433.6 1.4 pad_maximum_fusion.2
  434.9 0.6 fusion.61
  435.6 89.2 %all-reduce.3 = (f32[]{:T(128)}, f32[]{:T(128)}) all-reduce(f32[]{:T(128)} %get-tuple-element.20, f32[]{:T(128)} %get-tuple-element.19), channel_id=1, replica_groups=mesh['scan'=4,'slab'=64] {'scan','slab'}, use_global_device_ids=true, to_apply=%region_14.16 | all-reduce | flops 2 | bytes 16 | tf_op jit(solution)/shard_map/psum | solution.py:152
  526.1 7.8 %add_bitcast_fusion = f32[1,512,1024]{1,2,0:T(8,128)} fusion(f32[512,1024]{0,1:T(8,128)} %get-tuple-element.41, f32[512,1024]{0,1:T(8,128)} %get-tuple-element.38, f32[512,1024]{0,1:T(8,128)} %get-tuple-element.42, f32[512,1024]{0,1:T(8,128)} %get-tuple-element.40, f32[512,1024]{0,1:T(8,128)S(1)} %get-tuple-element.37, f32[512,1024]{0,1:T(8,128)} %get-tuple-element.39, ...), kind=kLoop, calls=%fused_computation.9 | loop fusion | flops 5767168 | bytes 16781312 | tf_op jit(solution)/shard_map/broadcast_in_dim | solution.py:158
  534.0 2.9 copy.72
  (72 shorter events, 1.8 us)
Async XLA Ops:
  0.6 13.3 %copy-start.7 = (s32[3]{0:T(128)S(1)}, s32[3]{0:T(128)}, u32[]{:S(2)}) copy-start(s32[3]{0:T(128)} %constant.79) | copy-start | bytes 40
  0.6 13.4 %copy-start.8 = (s32[3]{0:T(128)S(1)}, s32[3]{0:T(128)}, u32[]{:S(2)}) copy-start(s32[3]{0:T(128)} %constant.82) | copy-start | bytes 40
  0.7 10.2 %copy-start.2 = (s32[1,2,512,1]{2,3,1,0:T(1,128)S(1)}, s32[1,2,512,1]{2,3,1,0:T(1,128)}, u32[]{:S(2)}) copy-start(s32[1,2,512,1]{2,3,1,0:T(1,128)} %param.10) | copy-start | bytes 12292
  0.7 13.5 %copy-start.4 = (s32[1,2,512]{2,1,0:T(2,128)S(1)}, s32[1,2,512]{2,1,0:T(2,128)}, u32[]{:S(2)}) copy-start(s32[1,2,512]{2,1,0:T(2,128)} %param.11) | copy-start | bytes 12292
  3.6 47.5 %collective-permute-start = (f32[512,1024]{0,1:T(8,128)}, f32[512,1024]{0,1:T(8,128)}, u32[]{:S(2)}, u32[]{:S(2)}) collective-permute-start(f32[512,1024]{0,1:T(8,128)} %bitcast.6), channel_id=1, source_target_pairs={{64,0},{128,64},{192,128},{65,1},{129,65},{193,129},{66,2},{130,66... | collective-permute-start | bytes 6291464 | tf_op jit(solution)/shard_map/ppermute | solution.py:34
  4.9 56.4 %collective-permute-start.1 = (f32[512,1024]{0,1:T(8,128)}, f32[512,1024]{0,1:T(8,128)}, u32[]{:S(2)}, u32[]{:S(2)}) collective-permute-start(f32[512,1024]{0,1:T(8,128)} %bitcast.6), channel_id=1, source_target_pairs={{0,64},{64,128},{128,192},{1,65},{65,129},{129,193},{2,66},{66,130... | collective-permute-start | bytes 6291464 | tf_op jit(solution)/shard_map/ppermute | solution.py:34
  91.4 15.3 %copy-start.5 = (s32[1,512]{1,0:T(1,128)S(1)}, s32[1,512]{1,0:T(1,128)}, u32[]{:S(2)}) copy-start(s32[1,512]{1,0:T(1,128)} %param.12) | copy-start | bytes 6148
  91.4 15.4 %copy-start.6 = (f32[4]{0:T(128)S(1)}, f32[4]{0:T(128)}, u32[]{:S(2)}) copy-start(f32[4]{0:T(128)} %param.13) | copy-start | bytes 52
  91.4 15.4 %copy-start.1 = (f32[1,512]{1,0:T(1,128)S(1)}, f32[1,512]{1,0:T(1,128)}, u32[]{:S(2)}) copy-start(f32[1,512]{1,0:T(1,128)} %param.9) | copy-start | bytes 6148
  91.4 154.2 %all-to-all-start.1 = ((f32[2,64,12,1024]{3,0,2,1:T(2,128)}), f32[2,64,12,1024]{3,0,2,1:T(2,128)}, u32[]{:S(2)}, u32[]{:S(2)}) async-start(f32[2,64,12,1024]{3,0,2,1:T(2,128)} %copy.70), calls=%async_computation.1 | async-start | bytes 12582912 | tf_op jit(solution)/shard_map/all_to_all | solution.py:127
  106.9 194.1 %collective-permute-start.4 = (f32[512]{0:T(512)S(1)}, f32[512]{0:T(512)S(1)}, u32[]{:S(2)}, u32[]{:S(2)}) collective-permute-start(f32[512]{0:T(512)S(1)} %get-tuple-element.69), channel_id=1, source_target_pairs={{0,2},{1,3},{2,4},{3,5},{4,6},{5,7},{6,8},{7,9},{8,10},{9,11},{10,... | collective-permute-start | bytes 6152 | tf_op jit(solution)/shard_map/ppermute | solution.py:34
  110.1 190.8 %collective-permute-start.5 = (f32[512]{0:T(512)S(1)}, f32[512]{0:T(512)S(1)}, u32[]{:S(2)}, u32[]{:S(2)}) collective-permute-start(f32[512]{0:T(512)S(1)} %get-tuple-element.69), channel_id=1, source_target_pairs={{2,0},{3,1},{4,2},{5,3},{6,4},{7,5},{8,6},{9,7},{10,8},{11,9},{12,... | collective-permute-start | bytes 6152 | tf_op jit(solution)/shard_map/ppermute | solution.py:34
  112.0 18.7 %collective-permute-start.2 = (f32[1,1]{1,0:T(1,128)}, f32[1,1]{1,0:T(1,128)}, u32[]{:S(2)}, u32[]{:S(2)}) collective-permute-start(f32[1,1]{1,0:T(1,128)} %get-tuple-element.66), channel_id=1, source_target_pairs={{0,1},{1,2},{2,3},{3,4},{4,5},{5,6},{6,7},{7,8},{8,9},{9,10},{10,1... | collective-permute-start | bytes 20 | tf_op jit(solution)/shard_map/ppermute | solution.py:22
  116.9 13.9 %collective-permute-start.3 = (f32[1,1]{1,0:T(1,128)}, f32[1,1]{1,0:T(1,128)}, u32[]{:S(2)}, u32[]{:S(2)}) collective-permute-start(f32[1,1]{1,0:T(1,128)} %get-tuple-element.67), channel_id=1, source_target_pairs={{1,0},{2,1},{3,2},{4,3},{5,4},{6,5},{7,6},{8,7},{9,8},{10,9},{11,1... | collective-permute-start | bytes 20 | tf_op jit(solution)/shard_map/ppermute | solution.py:24
  276.2 3.3 copy-start
  301.0 18.8 %collective-permute-start.8 = (f32[512]{0:T(512)S(1)}, f32[512]{0:T(512)S(1)}, u32[]{:S(2)}, u32[]{:S(2)}) collective-permute-start(f32[512]{0:T(512)S(1)} %get-tuple-element.34), channel_id=1, source_target_pairs={{0,2},{1,3},{2,4},{3,5},{4,6},{5,7},{6,8},{7,9},{8,10},{9,11},{10,... | collective-permute-start | bytes 6152 | tf_op jit(solution)/shard_map/ppermute | solution.py:34
  304.1 15.7 %collective-permute-start.9 = (f32[512]{0:T(512)S(1)}, f32[512]{0:T(512)S(1)}, u32[]{:S(2)}, u32[]{:S(2)}) collective-permute-start(f32[512]{0:T(512)S(1)} %get-tuple-element.34), channel_id=1, source_target_pairs={{2,0},{3,1},{4,2},{5,3},{6,4},{7,5},{8,6},{9,7},{10,8},{11,9},{12,... | collective-permute-start | bytes 6152 | tf_op jit(solution)/shard_map/ppermute | solution.py:34
  306.0 9.2 %collective-permute-start.6 = (f32[1,1]{1,0:T(1,128)}, f32[1,1]{1,0:T(1,128)}, u32[]{:S(2)}, u32[]{:S(2)}) collective-permute-start(f32[1,1]{1,0:T(1,128)} %get-tuple-element.62), channel_id=1, source_target_pairs={{0,1},{1,2},{2,3},{3,4},{4,5},{5,6},{6,7},{7,8},{8,9},{9,10},{10,1... | collective-permute-start | bytes 20 | tf_op jit(solution)/shard_map/ppermute | solution.py:22
  313.3 5.2 collective-permute-start.7
  399.8 18.5 %collective-permute-start.12 = (f32[512]{0:T(512)S(1)}, f32[512]{0:T(512)S(1)}, u32[]{:S(2)}, u32[]{:S(2)}) collective-permute-start(f32[512]{0:T(512)S(1)} %get-tuple-element.32), channel_id=1, source_target_pairs={{0,2},{1,3},{2,4},{3,5},{4,6},{5,7},{6,8},{7,9},{8,10},{9,11},{10,... | collective-permute-start | bytes 6152 | tf_op jit(solution)/shard_map/ppermute | solution.py:34
  402.4 15.8 %collective-permute-start.13 = (f32[512]{0:T(512)S(1)}, f32[512]{0:T(512)S(1)}, u32[]{:S(2)}, u32[]{:S(2)}) collective-permute-start(f32[512]{0:T(512)S(1)} %get-tuple-element.32), channel_id=1, source_target_pairs={{2,0},{3,1},{4,2},{5,3},{6,4},{7,5},{8,6},{9,7},{10,8},{11,9},{12,... | collective-permute-start | bytes 6152 | tf_op jit(solution)/shard_map/ppermute | solution.py:34
  404.3 12.6 %collective-permute-start.10 = (f32[1,1]{1,0:T(1,128)}, f32[1,1]{1,0:T(1,128)}, u32[]{:S(2)}, u32[]{:S(2)}) collective-permute-start(f32[1,1]{1,0:T(1,128)} %get-tuple-element.56), channel_id=1, source_target_pairs={{0,1},{1,2},{2,3},{3,4},{4,5},{5,6},{6,7},{7,8},{8,9},{9,10},{10,1... | collective-permute-start | bytes 20 | tf_op jit(solution)/shard_map/ppermute | solution.py:22
  409.4 7.5 %collective-permute-start.11 = (f32[1,1]{1,0:T(1,128)}, f32[1,1]{1,0:T(1,128)}, u32[]{:S(2)}, u32[]{:S(2)}) collective-permute-start(f32[1,1]{1,0:T(1,128)} %get-tuple-element.57), channel_id=1, source_target_pairs={{1,0},{2,1},{3,2},{4,3},{5,4},{6,5},{7,6},{8,7},{9,8},{10,9},{11,1... | collective-permute-start | bytes 20 | tf_op jit(solution)/shard_map/ppermute | solution.py:24
  418.3 16.6 %collective-permute-start.16 = (f32[512]{0:T(512)S(1)}, f32[512]{0:T(512)S(1)}, u32[]{:S(2)}, u32[]{:S(2)}) collective-permute-start(f32[512]{0:T(512)S(1)} %get-tuple-element.29), channel_id=1, source_target_pairs={{0,2},{1,3},{2,4},{3,5},{4,6},{5,7},{6,8},{7,9},{8,10},{9,11},{10,... | collective-permute-start | bytes 6152 | tf_op jit(solution)/shard_map/ppermute | solution.py:34
  420.6 14.4 %collective-permute-start.17 = (f32[512]{0:T(512)S(1)}, f32[512]{0:T(512)S(1)}, u32[]{:S(2)}, u32[]{:S(2)}) collective-permute-start(f32[512]{0:T(512)S(1)} %get-tuple-element.29), channel_id=1, source_target_pairs={{2,0},{3,1},{4,2},{5,3},{6,4},{7,5},{8,6},{9,7},{10,8},{11,9},{12,... | collective-permute-start | bytes 6152 | tf_op jit(solution)/shard_map/ppermute | solution.py:34
  422.4 7.9 %collective-permute-start.14 = (f32[1,1]{1,0:T(1,128)}, f32[1,1]{1,0:T(1,128)}, u32[]{:S(2)}, u32[]{:S(2)}) collective-permute-start(f32[1,1]{1,0:T(1,128)} %get-tuple-element.52), channel_id=1, source_target_pairs={{0,1},{1,2},{2,3},{3,4},{4,5},{5,6},{6,7},{7,8},{8,9},{9,10},{10,1... | collective-permute-start | bytes 20 | tf_op jit(solution)/shard_map/ppermute | solution.py:22
  428.4 5.2 collective-permute-start.15
  526.1 7.9 %copy-start.3 = (f32[512]{0:T(512)}, f32[512]{0:T(512)S(1)}, u32[]{:S(2)}) copy-start(f32[512]{0:T(512)S(1)} %get-tuple-element.28) | copy-start | bytes 6148
where the time goes:
time: 542 us; the launch traced here: 537 us
  blocking collectives  190 us (35%)
  waiting for transfers between devices  128 us (24%)
  starting transfers between devices  81.8 us (15%)
  local copies, waits for them, and re-layouts  77.3 us (14%)
  other arithmetic  38.1 us (7%)
  matrix products  17 us (3%)
    psum x2, blocking collectives, on_device(): lax.psum((jnp.sum(direction * gradient), jnp.sum(curvature * direction *...  167 us
    all_to_all x1, waiting for transfers between devices, on_device(): lax.all_to_all(jnp.stack([forward_rows, backward_rows]), 'slab', split_ax...  114 us
    ppermute x10, starting transfers between devices, passed_along(): return lax.ppermute(block, axis, route)  23.8 us
    all_to_all x1, blocking collectives, on_device(): lax.all_to_all(request_table, 'slab', split_axis=1, concat_axis=1, tiled=...  23.1 us
    ppermute x4, starting transfers between devices, with_halo(): lax.ppermute(tail, axis, [(i, (i + 1) % count) for i in range(ends)])  23.1 us
    gather x1, local copies, waits for them, and re-layouts, on_device(): fetched = arrived[direction_ids, peer_ids, slot_ids]  21.5 us
    ppermute x4, starting transfers between devices, with_halo(): lax.ppermute(head, axis, [((i + 1) % count, i) for i in range(ends)])  19.6 us
    dot_general x8, matrix products, prefilter(): jnp.dot(window, matrix, preferred_element_type=jnp.float32, precision=lax...  17 us
  transfers between devices with their start and end apart: 19, of which 4 were waited for; matrix products, arithmetic and copies ran while one was open for 16% of the time, Pallas kernels for 0%

commit v1 on v0

--- a/solution.py
+++ b/solution.py
@@ -121,7 +121,12 @@
         .at[direction_ids, peer_ids, slot_ids]
         .set(wanted_rows)
     )
-    asked_rows = lax.all_to_all(request_table, "slab", split_axis=1, concat_axis=1, tiled=True)
+    asked_rows = jnp.concatenate(
+        lax.all_to_all(
+            jnp.stack(jnp.split(request_table, lax.axis_size("slab"), axis=1)), "slab", 0, 0
+        ),
+        axis=1,
+    )
     forward_rows = jnp.take(ahead_rows, asked_rows[0], axis=0)
     backward_rows = jnp.take(behind, asked_rows[1], axis=0)
     arrived = lax.all_to_all(

time: 542 us -> 543 us (level)
  local copies, waits for them, and re-layouts: 77.3 us -> 84.7 us
  waiting for transfers between devices: 128 us -> 121 us
    ppermute x10, waiting for transfers between devices: 8.4 us -> 0.65 us  [passed_along(): return lax.ppermute(block, axis, route)]
    split x0 -> x68, local copies, waits for them, and re-layouts: none -> 7.23 us  [on_device(): jnp.split(request_table, lax.axis_size('slab'), axis=1)]
  transfers between devices with their start and end apart: 19 -> 19, of which waited for: 4 -> 4; matrix products, arithmetic and copies ran while one was open for 16% -> 18% of each run, Pallas kernels for 0% -> 0%
where the time goes in v1:
time: 543 us; the launch traced here: 537 us
  blocking collectives  190 us (35%)
  waiting for transfers between devices  121 us (22%)
  local copies, waits for them, and re-layouts  84.7 us (16%)
  starting transfers between devices  81.6 us (15%)
  other arithmetic  38.1 us (7%)
  matrix products  17 us (3%)
    psum x2, blocking collectives, on_device(): lax.psum((jnp.sum(direction * gradient), jnp.sum(curvature * direction *...  167 us
    all_to_all x1, waiting for transfers between devices, on_device(): lax.all_to_all(jnp.stack([forward_rows, backward_rows]), 'slab', split_ax...  114 us
    ppermute x10, starting transfers between devices, passed_along(): return lax.ppermute(block, axis, route)  23.7 us
    all_to_all x1, blocking collectives, on_device(): lax.all_to_all(jnp.stack(jnp.split(request_table, lax.axis_size('slab'),...  23.1 us
    ppermute x4, starting transfers between devices, with_halo(): lax.ppermute(tail, axis, [(i, (i + 1) % count) for i in range(ends)])  23.1 us
    gather x1, local copies, waits for them, and re-layouts, on_device(): fetched = arrived[direction_ids, peer_ids, slot_ids]  21.5 us
    ppermute x4, starting transfers between devices, with_halo(): lax.ppermute(head, axis, [((i + 1) % count, i) for i in range(ends)])  19.6 us
    dot_general x8, matrix products, prefilter(): jnp.dot(window, matrix, preferred_element_type=jnp.float32, precision=lax...  17 us
  transfers between devices with their start and end apart: 19, of which 4 were waited for; matrix products, arithmetic and copies ran while one was open for 18% of the time, Pallas kernels for 0%

profile of v1, /device:TPU:1, one launch (start us, length us, event | category | flops | bytes accessed | tf_op | source)
XLA Modules:
  0.0 536.8 jit_solution(12122132153639234763)
XLA Ops:
  0.7 2.9 copy.713
  3.6 1.3 collective-permute-start
  4.9 6.0 %collective-permute-start.1 = (f32[512,1024]{0,1:T(8,128)}, f32[512,1024]{0,1:T(8,128)}, u32[]{:S(2)}, u32[]{:S(2)}) collective-permute-start(f32[512,1024]{0,1:T(8,128)} %bitcast.71), channel_id=1, source_target_pairs={{0,64},{64,128},{128,192},{1,65},{65,129},{129,193},{2,66},{66,130... | collective-permute-start | bytes 6291464 | tf_op jit(solution)/shard_map/ppermute | solution.py:34
  10.9 2.4 reduce-window.6
  13.3 0.3 slice_reduce_fusion
  14.2 4.3 scatter_custom_fusion
  26.6 23.1 %all_to_all.10 = s32[64,2,1,12]{3,1,2,0:T(2,128)S(1)} all-to-all(s32[64,2,1,12]{3,1,2,0:T(2,128)S(1)} %constant_dynamic-update-slice_fusion), channel_id=1, replica_groups=mesh['scan'=4,'slab'=64] {'slab'}, dimensions={0} | all-to-all | bytes 12288 | tf_op jit(solution)/shard_map/all_to_all | solution.py:125
  50.5 0.6 collective-permute-done
  51.1 1.9 copy.715
  53.0 3.6 gather_fusion.1
  56.6 4.6 reshape.170
  61.2 1.9 copy.718
  63.1 3.7 gather_fusion.2
  66.8 4.6 reshape.174
  71.4 3.8 select_bitcast_fusion
  75.3 4.2 pad_maximum_fusion
  79.4 12.0 %copy.719 = f32[2,64,12,1024]{3,0,2,1:T(2,128)} copy(f32[2,64,12,1024]{3,2,1,0:T(8,128)} %pad_maximum_fusion) | data formatting | bytes 12582912 | tf_op jit(solution)/shard_map/stack | solution.py:133
  91.4 15.3 %all-to-all-start.1 = ((f32[2,64,12,1024]{3,0,2,1:T(2,128)}), f32[2,64,12,1024]{3,0,2,1:T(2,128)}, u32[]{:S(2)}, u32[]{:S(2)}) async-start(f32[2,64,12,1024]{3,0,2,1:T(2,128)} %copy.719), calls=%async_computation.1 | async-start | bytes 12582912 | tf_op jit(solution)/shard_map/all_to_all | solution.py:132
  106.9 3.3 collective-permute-start.4
  110.1 1.3 collective-permute-start.5
  111.5 0.6 fusion.147
  112.0 4.8 collective-permute-start.2
  116.9 13.8 %collective-permute-start.3 = (f32[1,1]{1,0:T(1,128)}, f32[1,1]{1,0:T(1,128)}, u32[]{:S(2)}, u32[]{:S(2)}) collective-permute-start(f32[1,1]{1,0:T(1,128)} %get-tuple-element.135), channel_id=1, source_target_pairs={{1,0},{2,1},{3,2},{4,3},{5,4},{6,5},{7,6},{8,7},{9,8},{10,9},{11,1... | collective-permute-start | bytes 20 | tf_op jit(solution)/shard_map/ppermute | solution.py:24
  130.7 1.3 pad_maximum_fusion.8
  132.0 113.6 %all-to-all-done.1 = f32[2,64,12,1024]{3,0,2,1:T(2,128)} async-done(((f32[2,64,12,1024]{3,0,2,1:T(2,128)}), f32[2,64,12,1024]{3,0,2,1:T(2,128)}, u32[]{:S(2)}, u32[]{:S(2)}) %all-to-all-start.1) | async-done | bytes 6291488 | tf_op jit(solution)/shard_map/all_to_all | solution.py:132
  245.6 9.1 %copy.720 = f32[2,64,12,1024]{3,1,2,0:T(8,128)} copy(f32[2,64,12,1024]{3,0,2,1:T(2,128)} %all-to-all-done.1) | data formatting | bytes 12582912 | tf_op jit(solution)/shard_map/all_to_all | solution.py:132
  254.7 21.5 %gather_fusion = f32[1024,1024]{1,0:T(8,128)} fusion(f32[2,64,12,1024]{3,1,2,0:T(8,128)} %copy.720, s32[1024]{0:T(1024)S(1)} %bitcast.200), kind=kCustom, calls=%fused_computation.2 | custom fusion | bytes 8400896 | tf_op jit(solution)/shard_map/gather | solution.py:135
  276.2 3.3 fusion.35
  279.4 2.0 fusion.16
  281.4 2.0 fusion.19
  283.4 2.0 fusion.22
  285.4 2.0 fusion.25
  287.3 2.0 fusion.28
  289.3 2.0 fusion.31
  291.3 2.0 fusion.34
  293.3 0.5 fusion.139
  293.8 7.2 %add_reduce_fusion.2 = (f32[512]{0:T(512)S(1)}, f32[512]{0:T(512)S(1)}, f32[512,1024]{0,1:T(8,128)S(1)}, f32[512,1024]{0,1:T(8,128)}, f32[512,1024]{0,1:T(8,128)...) fusion(f32[512]{0:T(512)S(1)} %bitcast.208, f32[1,512,1024]{1,2,0:T(8,128)} %copy.713, ...), kind=kLoop, calls=%fused_computation.14 | loop fusion | flops 20970496 | bytes 18884608 | tf_op jit(solution)/shard_map/reduce_sum | solution.py:91
  301.0 3.1 collective-permute-start.8
  304.1 1.3 collective-permute-start.9
  305.4 0.6 fusion.146
  306.0 7.2 %collective-permute-start.6 = (f32[1,1]{1,0:T(1,128)}, f32[1,1]{1,0:T(1,128)}, u32[]{:S(2)}, u32[]{:S(2)}) collective-permute-start(f32[1,1]{1,0:T(1,128)} %get-tuple-element.130), channel_id=1, source_target_pairs={{0,1},{1,2},{2,3},{3,4},{4,5},{5,6},{6,7},{7,8},{8,9},{9,10},{10,1... | collective-permute-start | bytes 20 | tf_op jit(solution)/shard_map/ppermute | solution.py:22
  313.2 1.9 collective-permute-start.7
  315.2 3.3 collective-permute-done.7
  318.4 1.3 pad_maximum_fusion.6
  319.8 0.6 fusion.59
  320.4 78.0 %all-reduce.4 = (f32[]{:T(128)}, f32[]{:T(128)}) all-reduce(f32[]{:T(128)} %get-tuple-element.24, f32[]{:T(128)} %get-tuple-element.23), channel_id=1, replica_groups=mesh['scan'=4,'slab'=64] {'scan','slab'}, use_global_device_ids=true, to_apply=%region_8.10 | all-reduce | flops 2 | bytes 16 | tf_op jit(solution)/shard_map/psum | solution.py:157
  399.7 2.6 collective-permute-start.12
  402.2 1.3 collective-permute-start.13
  403.5 0.6 fusion.145
  404.1 5.1 collective-permute-start.10
  409.2 1.9 collective-permute-start.11
  411.2 5.5 %add_reduce_fusion = (f32[512]{0:T(512)S(1)}, f32[512]{0:T(512)S(1)}) fusion(f32[512,1024]{0,1:T(8,128)} %get-tuple-element.44, f32[512,1024]{0,1:T(8,128)} %get-tuple-element.43, f32[512,1024]{0,1:T(8,128)} %get-tuple-element.42, f32[512,1024]{0,1:T(8,128)} %get-tuple-element.41, f32[512]{0:T(512)S(1)} %get-tuple-element.35, ...), kind=kLoop, calls=%fused_computation.10 | loop fusion | flops 12581888 | bytes 14690304 | tf_op jit(solution)/shard_map/reduce_sum | solution.py:91
  416.7 1.3 pad_maximum_fusion.4
  418.1 2.2 collective-permute-start.16
  420.3 1.3 collective-permute-start.17
  421.6 0.6 fusion.144
  422.2 5.9 %collective-permute-start.14 = (f32[1,1]{1,0:T(1,128)}, f32[1,1]{1,0:T(1,128)}, u32[]{:S(2)}, u32[]{:S(2)}) collective-permute-start(f32[1,1]{1,0:T(1,128)} %get-tuple-element.120), channel_id=1, source_target_pairs={{0,1},{1,2},{2,3},{3,4},{4,5},{5,6},{6,7},{7,8},{8,9},{9,10},{10,1... | collective-permute-start | bytes 20 | tf_op jit(solution)/shard_map/ppermute | solution.py:22
  428.2 1.9 collective-permute-start.15
  430.1 3.3 collective-permute-done.15
  433.4 1.3 pad_maximum_fusion.2
  434.7 0.6 fusion.61
  435.3 89.2 %all-reduce.3 = (f32[]{:T(128)}, f32[]{:T(128)}) all-reduce(f32[]{:T(128)} %get-tuple-element.22, f32[]{:T(128)} %get-tuple-element.21), channel_id=1, replica_groups=mesh['scan'=4,'slab'=64] {'scan','slab'}, use_global_device_ids=true, to_apply=%region_14.16 | all-reduce | flops 2 | bytes 16 | tf_op jit(solution)/shard_map/psum | solution.py:157
  525.8 7.8 %add_bitcast_fusion = f32[1,512,1024]{1,2,0:T(8,128)} fusion(f32[512,1024]{0,1:T(8,128)} %get-tuple-element.43, f32[512,1024]{0,1:T(8,128)} %get-tuple-element.40, f32[512,1024]{0,1:T(8,128)} %get-tuple-element.44, f32[512,1024]{0,1:T(8,128)} %get-tuple-element.42, f32[512,1024]{0,1:T(8,128)S(1)} %get-tuple-element.39, f32[512,1024]{0,1:T(8,128)} %get-tuple-element.41, ...), kind=kLoop, calls=%fused_computation.9 | loop fusion | flops 5767168 | bytes 16781312 | tf_op jit(solution)/shard_map/broadcast_in_dim | solution.py:163
  533.7 2.9 copy.721
  (199 shorter events, 9.3 us)
Async XLA Ops:
  0.6 13.3 %copy-start.7 = (s32[3]{0:T(128)S(1)}, s32[3]{0:T(128)}, u32[]{:S(2)}) copy-start(s32[3]{0:T(128)} %constant.79) | copy-start | bytes 40
  0.6 13.4 %copy-start.8 = (s32[3]{0:T(128)S(1)}, s32[3]{0:T(128)}, u32[]{:S(2)}) copy-start(s32[3]{0:T(128)} %constant.82) | copy-start | bytes 40
  0.7 10.2 %copy-start.2 = (s32[1,2,512,1]{2,3,1,0:T(1,128)S(1)}, s32[1,2,512,1]{2,3,1,0:T(1,128)}, u32[]{:S(2)}) copy-start(s32[1,2,512,1]{2,3,1,0:T(1,128)} %param.10) | copy-start | bytes 12292
  0.7 13.5 %copy-start.4 = (s32[1,2,512]{2,1,0:T(2,128)S(1)}, s32[1,2,512]{2,1,0:T(2,128)}, u32[]{:S(2)}) copy-start(s32[1,2,512]{2,1,0:T(2,128)} %param.11) | copy-start | bytes 12292
  3.6 47.5 %collective-permute-start = (f32[512,1024]{0,1:T(8,128)}, f32[512,1024]{0,1:T(8,128)}, u32[]{:S(2)}, u32[]{:S(2)}) collective-permute-start(f32[512,1024]{0,1:T(8,128)} %bitcast.71), channel_id=1, source_target_pairs={{64,0},{128,64},{192,128},{65,1},{129,65},{193,129},{66,2},{130,66... | collective-permute-start | bytes 6291464 | tf_op jit(solution)/shard_map/ppermute | solution.py:34
  4.9 56.3 %collective-permute-start.1 = (f32[512,1024]{0,1:T(8,128)}, f32[512,1024]{0,1:T(8,128)}, u32[]{:S(2)}, u32[]{:S(2)}) collective-permute-start(f32[512,1024]{0,1:T(8,128)} %bitcast.71), channel_id=1, source_target_pairs={{0,64},{64,128},{128,192},{1,65},{65,129},{129,193},{2,66},{66,130... | collective-permute-start | bytes 6291464 | tf_op jit(solution)/shard_map/ppermute | solution.py:34
  91.4 15.3 %copy-start.5 = (s32[1,512]{1,0:T(1,128)S(1)}, s32[1,512]{1,0:T(1,128)}, u32[]{:S(2)}) copy-start(s32[1,512]{1,0:T(1,128)} %param.12) | copy-start | bytes 6148
  91.4 15.4 %copy-start.6 = (f32[4]{0:T(128)S(1)}, f32[4]{0:T(128)}, u32[]{:S(2)}) copy-start(f32[4]{0:T(128)} %param.13) | copy-start | bytes 52
  91.4 15.4 %copy-start.1 = (f32[1,512]{1,0:T(1,128)S(1)}, f32[1,512]{1,0:T(1,128)}, u32[]{:S(2)}) copy-start(f32[1,512]{1,0:T(1,128)} %param.9) | copy-start | bytes 6148
  91.4 154.2 %all-to-all-start.1 = ((f32[2,64,12,1024]{3,0,2,1:T(2,128)}), f32[2,64,12,1024]{3,0,2,1:T(2,128)}, u32[]{:S(2)}, u32[]{:S(2)}) async-start(f32[2,64,12,1024]{3,0,2,1:T(2,128)} %copy.719), calls=%async_computation.1 | async-start | bytes 12582912 | tf_op jit(solution)/shard_map/all_to_all | solution.py:132
  106.9 194.1 %collective-permute-start.4 = (f32[512]{0:T(512)S(1)}, f32[512]{0:T(512)S(1)}, u32[]{:S(2)}, u32[]{:S(2)}) collective-permute-start(f32[512]{0:T(512)S(1)} %get-tuple-element.137), channel_id=1, source_target_pairs={{0,2},{1,3},{2,4},{3,5},{4,6},{5,7},{6,8},{7,9},{8,10},{9,11},{10,... | collective-permute-start | bytes 6152 | tf_op jit(solution)/shard_map/ppermute | solution.py:34
  110.1 190.9 %collective-permute-start.5 = (f32[512]{0:T(512)S(1)}, f32[512]{0:T(512)S(1)}, u32[]{:S(2)}, u32[]{:S(2)}) collective-permute-start(f32[512]{0:T(512)S(1)} %get-tuple-element.137), channel_id=1, source_target_pairs={{2,0},{3,1},{4,2},{5,3},{6,4},{7,5},{8,6},{9,7},{10,8},{11,9},{12,... | collective-permute-start | bytes 6152 | tf_op jit(solution)/shard_map/ppermute | solution.py:34
  112.0 18.7 %collective-permute-start.2 = (f32[1,1]{1,0:T(1,128)}, f32[1,1]{1,0:T(1,128)}, u32[]{:S(2)}, u32[]{:S(2)}) collective-permute-start(f32[1,1]{1,0:T(1,128)} %get-tuple-element.134), channel_id=1, source_target_pairs={{0,1},{1,2},{2,3},{3,4},{4,5},{5,6},{6,7},{7,8},{8,9},{9,10},{10,1... | collective-permute-start | bytes 20 | tf_op jit(solution)/shard_map/ppermute | solution.py:22
  116.9 13.9 %collective-permute-start.3 = (f32[1,1]{1,0:T(1,128)}, f32[1,1]{1,0:T(1,128)}, u32[]{:S(2)}, u32[]{:S(2)}) collective-permute-start(f32[1,1]{1,0:T(1,128)} %get-tuple-element.135), channel_id=1, source_target_pairs={{1,0},{2,1},{3,2},{4,3},{5,4},{6,5},{7,6},{8,7},{9,8},{10,9},{11,1... | collective-permute-start | bytes 20 | tf_op jit(solution)/shard_map/ppermute | solution.py:24
  276.2 3.3 copy-start
  301.0 18.7 %collective-permute-start.8 = (f32[512]{0:T(512)S(1)}, f32[512]{0:T(512)S(1)}, u32[]{:S(2)}, u32[]{:S(2)}) collective-permute-start(f32[512]{0:T(512)S(1)} %get-tuple-element.36), channel_id=1, source_target_pairs={{0,2},{1,3},{2,4},{3,5},{4,6},{5,7},{6,8},{7,9},{8,10},{9,11},{10,... | collective-permute-start | bytes 6152 | tf_op jit(solution)/shard_map/ppermute | solution.py:34
  304.1 15.6 %collective-permute-start.9 = (f32[512]{0:T(512)S(1)}, f32[512]{0:T(512)S(1)}, u32[]{:S(2)}, u32[]{:S(2)}) collective-permute-start(f32[512]{0:T(512)S(1)} %get-tuple-element.36), channel_id=1, source_target_pairs={{2,0},{3,1},{4,2},{5,3},{6,4},{7,5},{8,6},{9,7},{10,8},{11,9},{12,... | collective-permute-start | bytes 6152 | tf_op jit(solution)/shard_map/ppermute | solution.py:34
  306.0 9.1 %collective-permute-start.6 = (f32[1,1]{1,0:T(1,128)}, f32[1,1]{1,0:T(1,128)}, u32[]{:S(2)}, u32[]{:S(2)}) collective-permute-start(f32[1,1]{1,0:T(1,128)} %get-tuple-element.130), channel_id=1, source_target_pairs={{0,1},{1,2},{2,3},{3,4},{4,5},{5,6},{6,7},{7,8},{8,9},{9,10},{10,1... | collective-permute-start | bytes 20 | tf_op jit(solution)/shard_map/ppermute | solution.py:22
  313.2 5.2 collective-permute-start.7
  399.7 18.4 %collective-permute-start.12 = (f32[512]{0:T(512)S(1)}, f32[512]{0:T(512)S(1)}, u32[]{:S(2)}, u32[]{:S(2)}) collective-permute-start(f32[512]{0:T(512)S(1)} %get-tuple-element.34), channel_id=1, source_target_pairs={{0,2},{1,3},{2,4},{3,5},{4,6},{5,7},{6,8},{7,9},{8,10},{9,11},{10,... | collective-permute-start | bytes 6152 | tf_op jit(solution)/shard_map/ppermute | solution.py:34
  402.2 15.8 %collective-permute-start.13 = (f32[512]{0:T(512)S(1)}, f32[512]{0:T(512)S(1)}, u32[]{:S(2)}, u32[]{:S(2)}) collective-permute-start(f32[512]{0:T(512)S(1)} %get-tuple-element.34), channel_id=1, source_target_pairs={{2,0},{3,1},{4,2},{5,3},{6,4},{7,5},{8,6},{9,7},{10,8},{11,9},{12,... | collective-permute-start | bytes 6152 | tf_op jit(solution)/shard_map/ppermute | solution.py:34
  404.1 12.6 %collective-permute-start.10 = (f32[1,1]{1,0:T(1,128)}, f32[1,1]{1,0:T(1,128)}, u32[]{:S(2)}, u32[]{:S(2)}) collective-permute-start(f32[1,1]{1,0:T(1,128)} %get-tuple-element.124), channel_id=1, source_target_pairs={{0,1},{1,2},{2,3},{3,4},{4,5},{5,6},{6,7},{7,8},{8,9},{9,10},{10,1... | collective-permute-start | bytes 20 | tf_op jit(solution)/shard_map/ppermute | solution.py:22
  409.2 7.5 %collective-permute-start.11 = (f32[1,1]{1,0:T(1,128)}, f32[1,1]{1,0:T(1,128)}, u32[]{:S(2)}, u32[]{:S(2)}) collective-permute-start(f32[1,1]{1,0:T(1,128)} %get-tuple-element.125), channel_id=1, source_target_pairs={{1,0},{2,1},{3,2},{4,3},{5,4},{6,5},{7,6},{8,7},{9,8},{10,9},{11,1... | collective-permute-start | bytes 20 | tf_op jit(solution)/shard_map/ppermute | solution.py:24
  418.1 16.6 %collective-permute-start.16 = (f32[512]{0:T(512)S(1)}, f32[512]{0:T(512)S(1)}, u32[]{:S(2)}, u32[]{:S(2)}) collective-permute-start(f32[512]{0:T(512)S(1)} %get-tuple-element.31), channel_id=1, source_target_pairs={{0,2},{1,3},{2,4},{3,5},{4,6},{5,7},{6,8},{7,9},{8,10},{9,11},{10,... | collective-permute-start | bytes 6152 | tf_op jit(solution)/shard_map/ppermute | solution.py:34
  420.3 14.4 %collective-permute-start.17 = (f32[512]{0:T(512)S(1)}, f32[512]{0:T(512)S(1)}, u32[]{:S(2)}, u32[]{:S(2)}) collective-permute-start(f32[512]{0:T(512)S(1)} %get-tuple-element.31), channel_id=1, source_target_pairs={{2,0},{3,1},{4,2},{5,3},{6,4},{7,5},{8,6},{9,7},{10,8},{11,9},{12,... | collective-permute-start | bytes 6152 | tf_op jit(solution)/shard_map/ppermute | solution.py:34
  422.2 7.9 %collective-permute-start.14 = (f32[1,1]{1,0:T(1,128)}, f32[1,1]{1,0:T(1,128)}, u32[]{:S(2)}, u32[]{:S(2)}) collective-permute-start(f32[1,1]{1,0:T(1,128)} %get-tuple-element.120), channel_id=1, source_target_pairs={{0,1},{1,2},{2,3},{3,4},{4,5},{5,6},{6,7},{7,8},{8,9},{9,10},{10,1... | collective-permute-start | bytes 20 | tf_op jit(solution)/shard_map/ppermute | solution.py:22
  428.2 5.2 collective-permute-start.15
  525.8 7.9 %copy-start.3 = (f32[512]{0:T(512)}, f32[512]{0:T(512)S(1)}, u32[]{:S(2)}) copy-start(f32[512]{0:T(512)S(1)} %get-tuple-element.30) | copy-start | bytes 6148
